TPU v7x, 32 devices: a whole 2x2x4 slice. The times are simulated.
32 devices in a mesh: dom: 8 (over z, core), four: 4 (over y, x).
Axes of the slice: x: 2, y: 2, z: 4, core: 2. Of those that a mesh axis runs over, the one named last changes fastest.
Arguments:
- velocity: float32 [3, 128, 18432], P(None, 'four', 'dom'), may hold values from -16 to 16
- partner: int32 [8, 4], P('dom'), may hold values from -1 to 7, as said below
- partner_side: int32 [8, 4], P('dom'), may hold values from -1 to 3, as said below
- flipped: int32 [8, 4], P('dom'), may hold values from 0 to 1, as said below
Outputs:
- new_velocity: float32 [3, 128, 18432], P(None, 'four', 'dom')
- residual: float32 [3, 128, 18432], P(None, 'four', 'dom')
Inputs may be any that keep to these rules, and one draw needn't show every extreme that they name: `partner`: sides are numbered 0 bottom, 1 right, 2 top, 3 left. Gluing is symmetric: if side s of partition p is glued to side s2 of partition q, then side s2 of q is glued to side s of p with the same flipped value. No side is glued to itself, and exactly 4 sides are walls (-1). `partner_side`: -1 exactly where partner is -1. `flipped`: 0 on wall sides.
All inputs are finite; a program needn't handle non-finite values.
Results may differ from a plain program's by a relative error of at most 0.0003.
Values sent between devices are 32-bit elements; how exact they have to be, the bound alone decides.
No kernel may reach another device: no remote copies, remote signals or barrier semaphores. Data moves between devices by JAX's collectives and lax.ppermute only.
A program may use at most 128 MiB of HBM per device.

v0:
```python
import math
import jax
import jax.numpy as jnp
import numpy as np
from jax import lax
from jax.sharding import PartitionSpec as P

ITERS = 4
REACTION = 2.0
WAVE_STEP = 0.0625
HIGHEST = lax.Precision.HIGHEST


def gll_tables():
    inner_near = math.sqrt(1.0 / 3.0 - 2.0 * math.sqrt(7.0) / 21.0)
    inner_far = math.sqrt(1.0 / 3.0 + 2.0 * math.sqrt(7.0) / 21.0)
    points = np.array([-1.0, -inner_far, -inner_near, inner_near, inner_far, 1.0])
    values = (63.0 * points**5 - 70.0 * points**3 + 15.0 * points) / 8.0
    weights = 2.0 / (30.0 * values * values)
    spacing = points[:, None] - points[None, :]
    same_point = spacing == 0.0
    derivative = np.where(
        same_point, 0.0, values[:, None] / (values[None, :] * np.where(same_point, 1.0, spacing))
    )
    end_fix = np.array([-7.5, 0.0, 0.0, 0.0, 0.0, 7.5])
    derivative = derivative + np.eye(6) * end_fix[None, :]
    stiffness = derivative.T @ (weights[:, None] * derivative)
    return (weights, derivative, stiffness)


def block_tables(blocks):
    weights, derivative, stiffness = gll_tables()
    identity = np.eye(blocks)
    weights_line = jnp.asarray(np.tile(weights, blocks), dtype=jnp.float32)
    deriv_block = jnp.asarray(np.kron(identity, derivative), dtype=jnp.float32)
    stiff_block = jnp.asarray(np.kron(identity, stiffness), dtype=jnp.float32)
    return (weights_line, deriv_block, stiff_block)


def fourier_tables(planes):
    plane_ids = jnp.arange(planes, dtype=jnp.int32)
    mode_ids = jnp.arange(planes, dtype=jnp.int32)
    waves = jnp.where(mode_ids < 2, 0, mode_ids // 2)
    phase_index = plane_ids[:, None] * waves[None, :] % planes
    angle = phase_index.astype(jnp.float32) * (2.0 * math.pi / planes)
    is_sine = (mode_ids % 2 == 1) & (mode_ids >= 2)
    basis = jnp.where(is_sine[None, :], jnp.sin(angle), jnp.cos(angle))
    alternating = jnp.where(plane_ids % 2 == 0, 1.0, -1.0).astype(jnp.float32)
    basis = jnp.where(mode_ids[None, :] == 1, alternating[:, None], basis)
    row_scale = jnp.where(mode_ids < 2, 1.0, 2.0).astype(jnp.float32) / planes
    forward = basis.T * row_scale[:, None]
    return (basis, forward)


def helmholtz_rates(mode_ids, planes):
    waves = jnp.where(mode_ids == 0, 0, jnp.where(mode_ids == 1, planes // 2, mode_ids // 2))
    scaled = waves.astype(jnp.float32) * WAVE_STEP
    return REACTION + scaled * scaled


def z_derivative(fields, mode_ids):
    waves = (mode_ids[0::2] // 2).astype(jnp.float32) * WAVE_STEP
    paired = fields.reshape(fields.shape[:1] + (-1, 2) + fields.shape[2:])
    cosine = paired[:, :, 0]
    sine = paired[:, :, 1]
    pair_waves = waves[None, :, None, None]
    result = jnp.stack([pair_waves * sine, -pair_waves * cosine], axis=2)
    return result.reshape(fields.shape)


def nonlinear_term(grids, mode_ids, deriv_block):
    along_x = jnp.matmul(grids[0:3], deriv_block.T, precision=HIGHEST)
    along_y = jnp.matmul(deriv_block, jnp.stack([grids[1], grids[3], grids[4]]), precision=HIGHEST)
    along_z = z_derivative(jnp.stack([grids[2], grids[4], grids[5]]), mode_ids)
    return -(along_x + along_y + along_z)


def pair_products(physical):
    return jnp.stack(
        [
            physical[0] * physical[0],
            physical[0] * physical[1],
            physical[0] * physical[2],
            physical[1] * physical[1],
            physical[1] * physical[2],
            physical[2] * physical[2],
        ]
    )


def junction_flags(side_nodes):
    positions = jnp.arange(side_nodes)
    at_end = (positions % 6 == 5) & (positions < side_nodes - 1)
    at_start = (positions % 6 == 0) & (positions > 0)
    return (at_end, at_start)


def dss_local(field):
    side_nodes = field.shape[-1]
    at_end, at_start = junction_flags(side_nodes)
    zero_col = jnp.zeros(field.shape[:-1] + (1,), field.dtype)
    from_right = jnp.concatenate([field[..., 1:], zero_col], axis=-1)
    from_left = jnp.concatenate([zero_col, field[..., :-1]], axis=-1)
    field = field + jnp.where(at_end, from_right, 0.0) + jnp.where(at_start, from_left, 0.0)
    zero_row = jnp.zeros(field.shape[:-2] + (1, side_nodes), field.dtype)
    from_below = jnp.concatenate([field[..., 1:, :], zero_row], axis=-2)
    from_above = jnp.concatenate([zero_row, field[..., :-1, :]], axis=-2)
    field = (
        field
        + jnp.where(at_end[:, None], from_below, 0.0)
        + jnp.where(at_start[:, None], from_above, 0.0)
    )
    return field


def side_values(grid):
    return jnp.stack(
        [grid[..., 0, :], grid[..., :, -1], grid[..., -1, :], grid[..., :, 0]], axis=-2
    )


def add_sides(grid, incoming):
    grid = grid.at[..., 0, :].add(incoming[..., 0, :])
    grid = grid.at[..., :, -1].add(incoming[..., 1, :])
    grid = grid.at[..., -1, :].add(incoming[..., 2, :])
    grid = grid.at[..., :, 0].add(incoming[..., 3, :])
    return grid


def edge_tables(partner_rows, side_nodes):
    positions = jnp.arange(side_nodes)
    rows_at = jnp.broadcast_to(positions[:, None], (side_nodes, side_nodes))
    cols_at = jnp.broadcast_to(positions[None, :], (side_nodes, side_nodes))
    on_side = jnp.stack(
        [rows_at == 0, cols_at == side_nodes - 1, rows_at == side_nodes - 1, cols_at == 0]
    )
    is_glued = (partner_rows >= 0)[..., :, None, None]
    wall_node = jnp.any(on_side & jnp.logical_not(is_glued), axis=-3)
    glued_node = jnp.any(on_side & is_glued, axis=-3)
    corner = ((rows_at == 0) | (rows_at == side_nodes - 1)) & (
        (cols_at == 0) | (cols_at == side_nodes - 1)
    )
    kept_node = jnp.logical_not(wall_node | corner)
    dirichlet_mask = kept_node.astype(jnp.float32)
    at_end, at_start = junction_flags(side_nodes)
    copies = jnp.where(at_end | at_start, 2.0, 1.0).astype(jnp.float32)
    weight = dirichlet_mask / (copies[:, None] * copies[None, :] * jnp.where(glued_node, 2.0, 1.0))
    return (dirichlet_mask, weight)


def apply_element(field, rates, weights_line, stiff_block):
    rows_part = jnp.matmul(stiff_block, field, precision=HIGHEST) * weights_line[None, :]
    cols_part = jnp.matmul(field, stiff_block, precision=HIGHEST) * weights_line[:, None]
    return rows_part + cols_part + rates * (weights_line[:, None] * weights_line[None, :]) * field


def inner_terms(weight, first_field, second_field):
    return jnp.sum(weight * first_field * second_field, axis=(-2, -1))


def shards(velocity, partner, partner_side, flipped):
    modes_here = velocity.shape[1]
    side_nodes = math.isqrt(velocity.shape[2])
    blocks = side_nodes // 6
    planes_all = modes_here * lax.axis_size("four")
    weights_line, deriv_block, stiff_block = block_tables(blocks)
    basis, forward = fourier_tables(planes_all)
    mode_ids = lax.axis_index("four") * modes_here + jnp.arange(modes_here, dtype=jnp.int32)
    mass_grid = weights_line[:, None] * weights_line[None, :]
    spread = lax.all_to_all(velocity, "four", split_axis=2, concat_axis=1, tiled=True)
    physical = jnp.einsum("jm,cmn->cjn", basis, spread, precision=HIGHEST)
    modal = jnp.einsum("mj,cjn->cmn", forward, pair_products(physical), precision=HIGHEST)
    returned = lax.all_to_all(modal, "four", split_axis=1, concat_axis=2, tiled=True)
    grids = returned.reshape(6, modes_here, side_nodes, side_nodes)
    nonlinear = nonlinear_term(grids, mode_ids, deriv_block)
    current = velocity.reshape(3, modes_here, side_nodes, side_nodes)
    local_rhs = mass_grid * (REACTION * current + nonlinear)
    partner_row = partner[0]
    side_row = partner_side[0]
    flip_row = flipped[0]
    dirichlet_mask, weight = edge_tables(partner, side_nodes)
    rates = helmholtz_rates(mode_ids, planes_all)[:, None, None]

    def assemble(field):
        joined = dss_local(field)
        edges = side_values(joined)
        leading = edges.shape[:2]
        packed = edges.reshape((1,) + leading + (4 * side_nodes,))
        piece = lax.all_gather(packed, "dom", axis=0, tiled=True)
        row_count = piece.shape[0]
        collected = []
        for side_index in range(4):
            offset_row = partner_row[side_index]
            inside = (offset_row >= 0) & (offset_row < row_count)
            chosen = lax.dynamic_index_in_dim(
                piece, jnp.clip(offset_row, 0, row_count - 1), 0, keepdims=False
            )
            segment = lax.dynamic_slice_in_dim(
                chosen, jnp.maximum(side_row[side_index], 0) * side_nodes, side_nodes, axis=2
            )
            segment = jnp.where(flip_row[side_index] == 1, segment[..., ::-1], segment)
            collected.append(jnp.where(inside, segment, 0.0))
        incoming = jnp.zeros(edges.shape, jnp.float32) + jnp.stack(collected, axis=2)
        return add_sides(joined, incoming)

    def operate(field):
        return dirichlet_mask * assemble(apply_element(field, rates, weights_line, stiff_block))

    def squares(residual):
        return lax.psum(inner_terms(weight, residual, residual), "dom")[..., None, None]

    def solve(rhs):
        solution = jnp.zeros_like(rhs)
        residual = rhs
        direction = rhs
        norm_now = squares(residual)
        for iteration in range(ITERS):
            image = operate(direction)
            alpha = (
                norm_now / lax.psum(inner_terms(weight, direction, image), "dom")[..., None, None]
            )
            solution = solution + alpha * direction
            residual = residual - alpha * image
            norm_next = squares(residual)
            direction = residual + norm_next / norm_now * direction
            norm_now = norm_next
        return (solution, residual)

    rhs_all = dirichlet_mask * assemble(local_rhs)
    results_each = [solve(rhs_all[component : component + 1]) for component in range(3)]
    solution = jnp.concatenate([outcome[0] for outcome in results_each], axis=0)
    residual = jnp.concatenate([outcome[1] for outcome in results_each], axis=0)
    new_velocity = solution.reshape(3, modes_here, side_nodes * side_nodes)
    return (new_velocity, residual.reshape(3, modes_here, side_nodes * side_nodes))


def solution(mesh):
    return jax.shard_map(
        shards,
        mesh=mesh,
        in_specs=(P(None, "four", "dom"), P("dom", None), P("dom", None), P("dom", None)),
        out_specs=(P(None, "four", "dom"), P(None, "four", "dom")),
        check_vma=False,
    )
```

profile of v0, /device:TPU:0, one launch (start us, length us, event | category | flops | bytes accessed | tf_op | source)
XLA Modules:
  0.0 1019.5 jit_solution(3872231014934521346)
XLA Ops:
  0.6 4.7 copy.6838
  5.3 5.6 reshape.2898
  10.9 5.2 all-to-all-start
  35.5 5.1 reshape.2899
  40.7 3.6 copy.6839
  50.6 4.4 all-to-all-start.1
  57.1 3.5 mul.537
  63.8 21.1 %all-to-all-done.1 = f32[6,128,576]{2,0,1:T(8,128)S(1)} async-done(((f32[6,128,576]{2,0,1:T(8,128)}), f32[6,128,576]{2,0,1:T(8,128)S(1)}, u32[]{:S(2)}, u32[]{:S(2)}) %all-to-all-start.1) | async-done | bytes 1769504 | tf_op jit(solution)/shard_map/all_to_all | solution.py:173
  112.2 8.1 fusion.218
  120.3 3.9 fusion.9
  135.2 15.8 %all_gather.39 = f32[8,3,32,192]{3,2,1,0:T(8,128)S(1)} all-gather(f32[1,3,32,192]{3,2,1,0:T(8,128)S(1)} %reshape.2780), channel_id=1, replica_groups=mesh['dom'=8,'four'=4] {'dom'}, dimensions={0}, use_global_device_ids=true | all-gather | bytes 663552 | tf_op jit(solution)/shard_map/all_gather | solution.py:189
  153.8 13.0 %scatter-add.174 = f32[3,32,48,48]{2,3,1,0:T(8,128)S(1)} dynamic-update-slice(f32[3,32,48,48]{2,3,1,0:T(8,128)S(1)} %select_add_fusion, f32[3,32,1,48]{2,3,1,0:T(8,128)} %copy.6860, s32[]{:T(128)} %constant.2451.clone.1, s32[]{:T(128)} %constant.2451.clone.1, s32[]{:T(128)} %constant.2451.clone.1, s32[]{:T(128)} %constant.2451.clone.1) | dynamic-update-slice | bytes 36868 | tf_op jit(solution)/shard_map/scatter-add | solution.py:123
  176.3 19.5 %scatter-add.176 = f32[3,32,48,48]{2,3,1,0:T(8,128)S(1)} dynamic-update-slice(f32[3,32,48,48]{2,3,1,0:T(8,128)S(1)} %scatter-add.175, f32[3,32,1,48]{2,3,1,0:T(8,128)} %copy.6864, s32[]{:T(128)} %constant.2451.clone.1, s32[]{:T(128)} %constant.2451.clone.1, s32[]{:T(128)} %constant.2452.clone.1, s32[]{:T(128)} %constant.2451.clone.1) | dynamic-update-slice | bytes 36868 | tf_op jit(solution)/shard_map/scatter-add | solution.py:125
  211.7 3.4 pad_maximum_fusion.3
  216.8 14.4 %all_gather.40 = f32[8,1,32,192]{3,2,1,0:T(8,128)S(1)} all-gather(f32[1,1,32,192]{3,2,1,0:T(8,128)S(1)} %reshape.2786), channel_id=1, replica_groups=mesh['dom'=8,'four'=4] {'dom'}, dimensions={0}, use_global_device_ids=true | all-gather | bytes 221184 | tf_op jit(solution)/shard_map/all_gather | solution.py:189
  241.6 5.3 scatter-add.184
  247.5 17.0 %all-reduce.57 = (f32[1,32]{1,0:T(1,128)S(1)}, f32[1,32]{1,0:T(1,128)S(1)}) all-reduce(f32[1,32]{1,0:T(1,128)S(1)} %bitcast.716, f32[1,32]{1,0:T(1,128)S(1)} %bitcast.715), channel_id=1, replica_groups=mesh['dom'=8,'four'=4] {'dom'}, use_global_device_ids=true, to_apply=%region_3.4 | all-reduce | flops 64 | bytes 512 | tf_op jit(solution)/shard_map/psum | solution.py:210
  265.0 13.6 %psum.170 = f32[1,32]{1,0:T(1,128)S(1)} all-reduce(f32[1,32]{1,0:T(1,128)S(1)} %bitcast.723), channel_id=1, replica_groups=mesh['dom'=8,'four'=4] {'dom'}, use_global_device_ids=true, to_apply=%region_7.8 | all-reduce | flops 32 | bytes 256 | tf_op jit(solution)/shard_map/psum | solution.py:210
  298.1 3.6 pad_maximum_fusion.4
  303.4 14.2 %all_gather.41 = f32[8,1,32,192]{3,2,1,0:T(8,128)S(1)} all-gather(f32[1,1,32,192]{3,2,1,0:T(8,128)S(1)} %reshape.2792), channel_id=1, replica_groups=mesh['dom'=8,'four'=4] {'dom'}, dimensions={0}, use_global_device_ids=true | all-gather | bytes 221184 | tf_op jit(solution)/shard_map/all_gather | solution.py:189
  330.5 5.8 scatter-add.190
  336.3 3.4 pad_maximum_fusion.7
  341.4 14.2 %all_gather.44 = f32[8,1,32,192]{3,2,1,0:T(8,128)S(1)} all-gather(f32[1,1,32,192]{3,2,1,0:T(8,128)S(1)} %reshape.2810), channel_id=1, replica_groups=mesh['dom'=8,'four'=4] {'dom'}, dimensions={0}, use_global_device_ids=true | all-gather | bytes 221184 | tf_op jit(solution)/shard_map/all_gather | solution.py:189
  366.1 5.3 scatter-add.210
  374.7 13.9 %psum.171 = f32[1,32]{1,0:T(1,128)S(1)} all-reduce(f32[1,32]{1,0:T(1,128)S(1)} %bitcast.719), channel_id=1, replica_groups=mesh['dom'=8,'four'=4] {'dom'}, use_global_device_ids=true, to_apply=%region_9.10 | all-reduce | flops 32 | bytes 256 | tf_op jit(solution)/shard_map/psum | solution.py:220
  391.2 14.0 %psum.172 = f32[1,32]{1,0:T(1,128)S(1)} all-reduce(f32[1,32]{1,0:T(1,128)S(1)} %bitcast.717), channel_id=1, replica_groups=mesh['dom'=8,'four'=4] {'dom'}, use_global_device_ids=true, to_apply=%region_11.12 | all-reduce | flops 32 | bytes 256 | tf_op jit(solution)/shard_map/psum | solution.py:210
  421.2 3.4 pad_maximum_fusion.10
  426.3 14.2 %all_gather.48 = f32[8,1,32,192]{3,2,1,0:T(8,128)S(1)} all-gather(f32[1,1,32,192]{3,2,1,0:T(8,128)S(1)} %reshape.2834), channel_id=1, replica_groups=mesh['dom'=8,'four'=4] {'dom'}, dimensions={0}, use_global_device_ids=true | all-gather | bytes 221184 | tf_op jit(solution)/shard_map/all_gather | solution.py:189
  444.9 3.3 scatter-add.234
  453.8 5.8 scatter-add.236
  459.6 3.5 pad_maximum_fusion.5
  464.7 14.2 %all_gather.42 = f32[8,1,32,192]{3,2,1,0:T(8,128)S(1)} all-gather(f32[1,1,32,192]{3,2,1,0:T(8,128)S(1)} %reshape.2798), channel_id=1, replica_groups=mesh['dom'=8,'four'=4] {'dom'}, dimensions={0}, use_global_device_ids=true | all-gather | bytes 221184 | tf_op jit(solution)/shard_map/all_gather | solution.py:189
  489.3 5.3 scatter-add.196
  498.2 13.9 %all-reduce.56 = (f32[1,32]{1,0:T(1,128)S(1)}, f32[1,32]{1,0:T(1,128)S(1)}, f32[1,32]{1,0:T(1,128)S(1)}) all-reduce(f32[1,32]{1,0:T(1,128)S(1)} %bitcast.712, f32[1,32]{1,0:T(1,128)S(1)} %bitcast.711, f32[1,32]{1,0:T(1,128)S(1)} %bitcast.713), channel_id=1, replica_groups=mesh['dom'=8,'four'=4] {'dom'}, use_global_device_ids=true, to_apply=%region_35.36 | all-reduce | flops 96 | bytes 768 | tf_op jit(solution)/shard_map/psum | solution.py:210
  512.1 3.4 fusion.20
  515.5 13.8 %all-reduce.55 = (f32[1,32]{1,0:T(1,128)S(1)}, f32[1,32]{1,0:T(1,128)S(1)}, f32[1,32]{1,0:T(1,128)S(1)}, f32[1,32]{1,0:T(1,128)S(1)}) all-reduce(f32[1,32]{1,0:T(1,128)S(1)} %bitcast.704, f32[1,32]{1,0:T(1,128)S(1)} %bitcast.703, f32[1,32]{1,0:T(1,128)S(1)} %bitcast.702, ...), channel_id=1, replica_groups=mesh['dom'=8,'four'=4] {'dom'}, use_global_device_ids=true, to_apply=%region_39.40 | all-reduce | flops 128 | bytes 1024 | tf_op jit(solution)/shard_map/psum | solution.py:210
  549.5 3.4 pad_maximum_fusion.11
  554.6 14.6 %all_gather.49 = f32[8,1,32,192]{3,2,1,0:T(8,128)S(1)} all-gather(f32[1,1,32,192]{3,2,1,0:T(8,128)S(1)} %reshape.2840), channel_id=1, replica_groups=mesh['dom'=8,'four'=4] {'dom'}, dimensions={0}, use_global_device_ids=true | all-gather | bytes 221184 | tf_op jit(solution)/shard_map/all_gather | solution.py:189
  582.3 5.8 scatter-add.244
  588.2 3.5 pad_maximum_fusion.6
  593.3 14.2 %all_gather.43 = f32[8,1,32,192]{3,2,1,0:T(8,128)S(1)} all-gather(f32[1,1,32,192]{3,2,1,0:T(8,128)S(1)} %reshape.2804), channel_id=1, replica_groups=mesh['dom'=8,'four'=4] {'dom'}, dimensions={0}, use_global_device_ids=true | all-gather | bytes 221184 | tf_op jit(solution)/shard_map/all_gather | solution.py:189
  618.1 5.3 scatter-add.204
  627.3 14.1 %psum.178 = f32[1,32]{1,0:T(1,128)S(1)} all-reduce(f32[1,32]{1,0:T(1,128)S(1)} %bitcast.720), channel_id=1, replica_groups=mesh['dom'=8,'four'=4] {'dom'}, use_global_device_ids=true, to_apply=%region_23.24 | all-reduce | flops 32 | bytes 256 | tf_op jit(solution)/shard_map/psum | solution.py:210
  651.7 3.4 pad_maximum_fusion.8
  656.8 14.2 %all_gather.45 = f32[8,1,32,192]{3,2,1,0:T(8,128)S(1)} all-gather(f32[1,1,32,192]{3,2,1,0:T(8,128)S(1)} %reshape.2816), channel_id=1, replica_groups=mesh['dom'=8,'four'=4] {'dom'}, dimensions={0}, use_global_device_ids=true | all-gather | bytes 221184 | tf_op jit(solution)/shard_map/all_gather | solution.py:189
  684.2 5.8 scatter-add.216
  693.0 13.9 %psum.179 = f32[1,32]{1,0:T(1,128)S(1)} all-reduce(f32[1,32]{1,0:T(1,128)S(1)} %bitcast.724), channel_id=1, replica_groups=mesh['dom'=8,'four'=4] {'dom'}, use_global_device_ids=true, to_apply=%region_25.26 | all-reduce | flops 32 | bytes 256 | tf_op jit(solution)/shard_map/psum | solution.py:220
  709.6 13.8 %psum.180 = f32[1,32]{1,0:T(1,128)S(1)} all-reduce(f32[1,32]{1,0:T(1,128)S(1)} %bitcast.718), channel_id=1, replica_groups=mesh['dom'=8,'four'=4] {'dom'}, use_global_device_ids=true, to_apply=%region_27.28 | all-reduce | flops 32 | bytes 256 | tf_op jit(solution)/shard_map/psum | solution.py:210
  741.0 14.2 %all_gather.46 = f32[8,1,32,192]{3,2,1,0:T(8,128)S(1)} all-gather(f32[1,1,32,192]{3,2,1,0:T(8,128)S(1)} %reshape.2822), channel_id=1, replica_groups=mesh['dom'=8,'four'=4] {'dom'}, dimensions={0}, use_global_device_ids=true | all-gather | bytes 221184 | tf_op jit(solution)/shard_map/all_gather | solution.py:189
  767.2 5.8 scatter-add.224
  776.1 13.9 %all-reduce.54 = (f32[1,32]{1,0:T(1,128)S(1)}, f32[1,32]{1,0:T(1,128)S(1)}) all-reduce(f32[1,32]{1,0:T(1,128)S(1)} %bitcast.706, f32[1,32]{1,0:T(1,128)S(1)} %bitcast.721), channel_id=1, replica_groups=mesh['dom'=8,'four'=4] {'dom'}, use_global_device_ids=true, to_apply=%region_41.42 | all-reduce | flops 64 | bytes 512 | tf_op jit(solution)/shard_map/psum | solution.py:220
  790.0 3.3 fusion.23
  793.4 14.1 %all-reduce.53 = (f32[1,32]{1,0:T(1,128)S(1)}, f32[1,32]{1,0:T(1,128)S(1)}) all-reduce(f32[1,32]{1,0:T(1,128)S(1)} %bitcast.709, f32[1,32]{1,0:T(1,128)S(1)} %bitcast.708), channel_id=1, replica_groups=mesh['dom'=8,'four'=4] {'dom'}, use_global_device_ids=true, to_apply=%region_43.44 | all-reduce | flops 64 | bytes 512 | tf_op jit(solution)/shard_map/psum | solution.py:210
  827.2 3.4 pad_maximum_fusion.12
  832.3 14.2 %all_gather.50 = f32[8,1,32,192]{3,2,1,0:T(8,128)S(1)} all-gather(f32[1,1,32,192]{3,2,1,0:T(8,128)S(1)} %reshape.2846), channel_id=1, replica_groups=mesh['dom'=8,'four'=4] {'dom'}, dimensions={0}, use_global_device_ids=true | all-gather | bytes 221184 | tf_op jit(solution)/shard_map/all_gather | solution.py:189
  859.6 5.8 scatter-add.250
  871.8 14.2 %all_gather.47 = f32[8,1,32,192]{3,2,1,0:T(8,128)S(1)} all-gather(f32[1,1,32,192]{3,2,1,0:T(8,128)S(1)} %reshape.2828), channel_id=1, replica_groups=mesh['dom'=8,'four'=4] {'dom'}, dimensions={0}, use_global_device_ids=true | all-gather | bytes 221184 | tf_op jit(solution)/shard_map/all_gather | solution.py:189
  898.5 4.8 scatter-add.230
  909.7 13.9 %psum.189 = f32[1,32]{1,0:T(1,128)S(1)} all-reduce(f32[1,32]{1,0:T(1,128)S(1)} %bitcast.722), channel_id=1, replica_groups=mesh['dom'=8,'four'=4] {'dom'}, use_global_device_ids=true, to_apply=%region_45.46 | all-reduce | flops 32 | bytes 256 | tf_op jit(solution)/shard_map/psum | solution.py:220
  928.0 13.8 %psum.190 = f32[1,32]{1,0:T(1,128)S(1)} all-reduce(f32[1,32]{1,0:T(1,128)S(1)} %bitcast.714), channel_id=1, replica_groups=mesh['dom'=8,'four'=4] {'dom'}, use_global_device_ids=true, to_apply=%region_47.48 | all-reduce | flops 32 | bytes 256 | tf_op jit(solution)/shard_map/psum | solution.py:210
  955.5 14.2 %all_gather.51 = f32[8,1,32,192]{3,2,1,0:T(8,128)S(1)} all-gather(f32[1,1,32,192]{3,2,1,0:T(8,128)S(1)} %reshape.2852), channel_id=1, replica_groups=mesh['dom'=8,'four'=4] {'dom'}, dimensions={0}, use_global_device_ids=true | all-gather | bytes 221184 | tf_op jit(solution)/shard_map/all_gather | solution.py:189
  978.0 5.3 scatter-add.256
  985.2 14.2 %all-reduce.52 = (f32[1,32]{1,0:T(1,128)S(1)}, f32[1,32]{1,0:T(1,128)S(1)}, f32[1,32]{1,0:T(1,128)S(1)}) all-reduce(f32[1,32]{1,0:T(1,128)S(1)} %bitcast.710, f32[1,32]{1,0:T(1,128)S(1)} %bitcast.707, f32[1,32]{1,0:T(1,128)S(1)} %bitcast.705), channel_id=1, replica_groups=mesh['dom'=8,'four'=4] {'dom'}, use_global_device_ids=true, to_apply=%region_49.50 | all-reduce | flops 96 | bytes 768 | tf_op jit(solution)/shard_map/psum | solution.py:220
  1003.3 3.4 multiply_subtract_fusion.1
  (571 shorter events, 409.9 us)
Async XLA Ops:
  5.3 10.8 %copy-start.43 = (s32[1,4]{1,0:T(1,128)S(1)}, s32[1,4]{1,0:T(1,128)}, u32[]{:S(2)}) copy-start(s32[1,4]{1,0:T(1,128)} %param.112) | copy-start | bytes 52
  5.3 10.8 %copy-start.42 = (s32[1,4]{1,0:T(1,128)S(1)}, s32[1,4]{1,0:T(1,128)}, u32[]{:S(2)}) copy-start(s32[1,4]{1,0:T(1,128)} %param.113) | copy-start | bytes 52
  5.3 23.0 %copy-start.44 = (s32[1,4]{1,0:T(1,128)S(1)}, s32[1,4]{1,0:T(1,128)}, u32[]{:S(2)}) copy-start(s32[1,4]{1,0:T(1,128)} %param.114) | copy-start | bytes 52
  10.9 20.9 %all-to-all-start = ((f32[4,1,55296]{2,1,0:T(1,128)}), f32[4,1,55296]{2,1,0:T(1,128)S(1)}, u32[]{:S(2)}, u32[]{:S(2)}) async-start(f32[4,1,55296]{2,1,0:T(1,128)} %reshape.2898), calls=%async_computation | async-start | bytes 1769472 | tf_op jit(solution)/shard_map/all_to_all | solution.py:170
  50.6 34.3 %all-to-all-start.1 = ((f32[6,128,576]{2,0,1:T(8,128)}), f32[6,128,576]{2,0,1:T(8,128)S(1)}, u32[]{:S(2)}, u32[]{:S(2)}) async-start(f32[6,128,576]{2,0,1:T(8,128)} %copy.6841), calls=%async_computation.1 | async-start | bytes 5242880 | tf_op jit(solution)/shard_map/all_to_all | solution.py:173
  60.6 3.2 copy-start.40
  104.5 2.5 copy-start.38
  108.9 3.3 copy-start.41
  112.2 8.1 copy-start.23
  112.2 8.1 copy-start.24
  198.5 0.7 copy-start.33
  199.3 4.2 copy-start.21
  203.5 0.7 copy-start.32
  203.7 79.4 %copy-start.17 = (f32[1,32,48,48]{2,3,1,0:T(8,128)}, f32[1,32,48,48]{2,3,1,0:T(8,128)S(1)}, u32[]{:S(2)}) copy-start(f32[1,32,48,48]{2,3,1,0:T(8,128)S(1)} %get-tuple-element.673) | copy-start | bytes 884740
  278.9 4.2 copy-start.6
  280.7 2.4 copy-start.35
  280.7 2.4 copy-start.36
  288.8 3.0 copy-start.3
  405.3 3.5 copy-start.22
  406.9 2.9 copy-start.8
  412.0 3.0 copy-start
  530.9 5.9 copy-start.20
  530.9 2.6 copy-start.31
  535.2 3.1 copy-start.9
  540.4 2.9 copy-start.1
  641.7 2.6 copy-start.5
  646.2 0.9 copy-start.4
  725.0 2.6 copy-start.16
  764.6 25.4 %copy-start.2 = (f32[1,32,48,48]{2,1,3,0:T(8,128)S(1)}, f32[1,32,48,48]{2,1,3,0:T(8,128)}, u32[]{:S(2)}) copy-start(f32[1,32,48,48]{2,1,3,0:T(8,128)} %constant_dynamic-update-slice_fusion.6) | copy-start | bytes 884740
  793.4 16.8 %copy-start.26 = (f32[1,32,48,48]{2,1,3,0:T(8,128)S(1)}, f32[1,32,48,48]{2,1,3,0:T(8,128)}, u32[]{:S(2)}) copy-start(f32[1,32,48,48]{2,1,3,0:T(8,128)} %get-tuple-element.663) | copy-start | bytes 884740
  810.2 2.5 copy-start.10
  810.2 2.5 copy-start.28
  811.1 5.5 copy-start.18
  820.5 2.0 copy-start.13
  821.0 2.9 copy-start.11
  923.6 2.9 copy-start.29
  923.6 2.9 copy-start.30
  943.1 2.7 copy-start.14
  975.6 23.7 %copy-start.7 = (f32[1,32,48,48]{2,1,3,0:T(8,128)S(1)}, f32[1,32,48,48]{2,1,3,0:T(8,128)}, u32[]{:S(2)}) copy-start(f32[1,32,48,48]{2,1,3,0:T(8,128)} %copy-done.6) | copy-start | bytes 884740
  999.3 3.9 copy-start.12
  999.3 3.9 copy-start.15
  999.4 3.9 copy-start.19
  999.4 3.9 copy-start.25
  999.4 3.9 copy-start.27
  999.4 3.9 copy-start.34
  999.4 3.9 copy-start.37
  1008.9 3.2 copy-start.39
where the time goes:
time: 1030 us; the launch traced here: 1020 us
  blocking collectives  385 us (37%)
  local copies, waits for them, and re-layouts  363 us (35%)
  other arithmetic  185 us (18%)
  matrix products  39.1 us (4%)
  waiting for transfers between devices  21.1 us (2%)
  between operations  16 us (2%)
    all_gather x13, blocking collectives, assemble(): piece = lax.all_gather(packed, 'dom', axis=0, tiled=True)  187 us
    psum x9, blocking collectives, squares(): lax.psum(inner_terms(weight, residual, residual), 'dom')[..., None, None]  128 us
    scatter-add x14, local copies, waits for them, and re-layouts, add_sides(): grid = grid.at[..., -1, :].add(incoming[..., 2, :])  88.5 us
    psum x5, blocking collectives, solve(): lax.psum(inner_terms(weight, direction, image), 'dom')[..., None, None]  69.9 us
    another operation x44, local copies, waits for them, and re-layouts  61.5 us
    another operation x46, local copies, waits for them, and re-layouts, side_values(): jnp.stack([grid[..., 0, :], grid[..., :, -1], grid[..., -1, :], grid[...,...  51.1 us
    scatter-add x13, local copies, waits for them, and re-layouts, add_sides(): grid = grid.at[..., 0, :].add(incoming[..., 0, :])  46.2 us
    another operation x13, other arithmetic, side_values(): jnp.stack([grid[..., 0, :], grid[..., :, -1], grid[..., -1, :], grid[...,...  37.4 us
  transfers between devices with their start and end apart: 2, of which 1 were waited for; matrix products, arithmetic and copies ran while one was open for 1% of the time, Pallas kernels for 0%

commit v1 on v0

--- a/solution.py
+++ b/solution.py
@@ -207,7 +207,9 @@
         return dirichlet_mask * assemble(apply_element(field, rates, weights_line, stiff_block))
 
     def squares(residual):
-        return lax.psum(inner_terms(weight, residual, residual), "dom")[..., None, None]
+        return jnp.sum(lax.all_gather(inner_terms(weight, residual, residual), "dom"), axis=0)[
+            ..., None, None
+        ]
 
     def solve(rhs):
         solution = jnp.zeros_like(rhs)

time: 1030 us -> 1050 us (1.019)
    psum x9 -> x0, blocking collectives: 128 us -> none  [squares(): lax.psum(inner_terms(weight, residual, residual), 'dom')[..., None, None]]
    unnamed x0 -> x9, blocking collectives: none -> 128 us
    unnamed x104 -> x143, local copies, waits for them, and re-layouts: 32.4 us -> 33.8 us
where the time goes in v1:
time: 1050 us; the launch traced here: 1040 us
  blocking collectives  385 us (37%)
  local copies, waits for them, and re-layouts  371 us (35%)
  other arithmetic  186 us (18%)
  matrix products  39.9 us (4%)
  waiting for transfers between devices  29.1 us (3%)
  between operations  16.2 us (2%)
    all_gather x13, blocking collectives, assemble(): piece = lax.all_gather(packed, 'dom', axis=0, tiled=True)  187 us
    unnamed x9, blocking collectives  128 us
    scatter-add x14, local copies, waits for them, and re-layouts, add_sides(): grid = grid.at[..., -1, :].add(incoming[..., 2, :])  88.5 us
    psum x5, blocking collectives, solve(): lax.psum(inner_terms(weight, direction, image), 'dom')[..., None, None]  69.8 us
    another operation x44, local copies, waits for them, and re-layouts  61.1 us
    another operation x46, local copies, waits for them, and re-layouts, side_values(): jnp.stack([grid[..., 0, :], grid[..., :, -1], grid[..., -1, :], grid[...,...  50.6 us
    scatter-add x13, local copies, waits for them, and re-layouts, add_sides(): grid = grid.at[..., 0, :].add(incoming[..., 0, :])  45.8 us
    another operation x13, other arithmetic, side_values(): jnp.stack([grid[..., 0, :], grid[..., :, -1], grid[..., -1, :], grid[...,...  37.5 us
  transfers between devices with their start and end apart: 2, of which 1 were waited for; matrix products, arithmetic and copies ran while one was open for 1% of the time, Pallas kernels for 0%

profile of v1, /device:TPU:0, one launch (start us, length us, event | category | flops | bytes accessed | tf_op | source)
XLA Modules:
  0.0 1036.9 jit_solution(14980765914034609908)
XLA Ops:
  0.6 4.7 copy.6838
  5.3 5.7 reshape.2967
  11.0 5.3 all-to-all-start
  37.2 4.1 reduce.154
  41.3 5.1 reshape.2968
  46.4 3.6 copy.6839
  56.4 4.7 all-to-all-start.1
  63.1 29.1 %all-to-all-done.1 = f32[6,128,576]{2,0,1:T(8,128)} async-done(((f32[6,128,576]{2,0,1:T(8,128)}), f32[6,128,576]{2,0,1:T(8,128)}, u32[]{:S(2)}, u32[]{:S(2)}) %all-to-all-start.1) | async-done | bytes 1769504 | tf_op jit(solution)/shard_map/all_to_all | solution.py:173
  123.0 8.1 fusion.218
  131.2 3.7 fusion.9
  145.8 16.2 %all_gather.111 = f32[8,3,32,192]{3,2,1,0:T(8,128)S(1)} all-gather(f32[1,3,32,192]{3,2,1,0:T(8,128)S(1)} %reshape.2753), channel_id=1, replica_groups=mesh['dom'=8,'four'=4] {'dom'}, dimensions={0}, use_global_device_ids=true | all-gather | bytes 663552 | tf_op jit(solution)/shard_map/all_gather | solution.py:189
  164.5 12.4 %scatter-add.174 = f32[3,32,48,48]{2,3,1,0:T(8,128)S(1)} dynamic-update-slice(f32[3,32,48,48]{2,3,1,0:T(8,128)S(1)} %select_add_fusion, f32[3,32,1,48]{2,3,1,0:T(8,128)} %copy.6860, s32[]{:T(128)} %constant.2451.clone.1, s32[]{:T(128)} %constant.2451.clone.1, s32[]{:T(128)} %constant.2451.clone.1, s32[]{:T(128)} %constant.2451.clone.1) | dynamic-update-slice | bytes 36868 | tf_op jit(solution)/shard_map/scatter-add | solution.py:123
  186.7 19.5 %scatter-add.176 = f32[3,32,48,48]{2,3,1,0:T(8,128)S(1)} dynamic-update-slice(f32[3,32,48,48]{2,3,1,0:T(8,128)S(1)} %scatter-add.175, f32[3,32,1,48]{2,3,1,0:T(8,128)} %copy.6864, s32[]{:T(128)} %constant.2451.clone.1, s32[]{:T(128)} %constant.2451.clone.1, s32[]{:T(128)} %constant.2452.clone.1, s32[]{:T(128)} %constant.2451.clone.1) | dynamic-update-slice | bytes 36868 | tf_op jit(solution)/shard_map/scatter-add | solution.py:125
  223.1 14.3 %all_gather.114 = f32[8,1,32,192]{3,2,1,0:T(8,128)S(1)} all-gather(f32[1,1,32,192]{3,2,1,0:T(8,128)S(1)} %reshape.2759), channel_id=1, replica_groups=mesh['dom'=8,'four'=4] {'dom'}, dimensions={0}, use_global_device_ids=true | all-gather | bytes 221184 | tf_op jit(solution)/shard_map/all_gather | solution.py:189
  245.7 5.3 scatter-add.184
  251.9 17.0 %all-reduce.69 = (f32[256]{0:T(256)S(1)}, f32[32]{0:T(128)S(1)}) all-reduce(f32[256]{0:T(256)S(1)} %dynamic-update-slice.156, f32[32]{0:T(128)S(1)} %get-tuple-element.626), channel_id=2, replica_groups=mesh['dom'=8,'four'=4] {'dom'}, use_global_device_ids=true, to_apply=%add.52 | all-reduce | flops 288 | bytes 2304
  269.7 14.0 %all-reduce.53 = f32[256]{0:T(256)S(1)} all-reduce(f32[256]{0:T(256)S(1)} %dynamic-update-slice.157), channel_id=3, replica_groups=mesh['dom'=8,'four'=4] {'dom'}, use_global_device_ids=true, to_apply=%add.53 | all-reduce | flops 256 | bytes 2048
  301.9 3.5 pad_maximum_fusion.7
  307.1 14.2 %all_gather.126 = f32[8,1,32,192]{3,2,1,0:T(8,128)S(1)} all-gather(f32[1,1,32,192]{3,2,1,0:T(8,128)S(1)} %reshape.2783), channel_id=1, replica_groups=mesh['dom'=8,'four'=4] {'dom'}, dimensions={0}, use_global_device_ids=true | all-gather | bytes 221184 | tf_op jit(solution)/shard_map/all_gather | solution.py:189
  331.7 5.3 scatter-add.210
  340.2 3.4 pad_maximum_fusion.4
  345.3 14.2 %all_gather.117 = f32[8,1,32,192]{3,2,1,0:T(8,128)S(1)} all-gather(f32[1,1,32,192]{3,2,1,0:T(8,128)S(1)} %reshape.2765), channel_id=1, replica_groups=mesh['dom'=8,'four'=4] {'dom'}, dimensions={0}, use_global_device_ids=true | all-gather | bytes 221184 | tf_op jit(solution)/shard_map/all_gather | solution.py:189
  372.4 5.8 scatter-add.190
  381.6 13.9 %psum.85 = f32[32]{0:T(128)S(1)} all-reduce(f32[32]{0:T(128)S(1)} %get-tuple-element.636), channel_id=1, replica_groups=mesh['dom'=8,'four'=4] {'dom'}, use_global_device_ids=true, to_apply=%region_9.10 | all-reduce | flops 32 | bytes 256 | tf_op jit(solution)/shard_map/psum | solution.py:222
  398.3 13.8 %all-reduce.54 = f32[256]{0:T(256)S(1)} all-reduce(f32[256]{0:T(256)S(1)} %dynamic-update-slice.158), channel_id=4, replica_groups=mesh['dom'=8,'four'=4] {'dom'}, use_global_device_ids=true, to_apply=%add.54 | all-reduce | flops 256 | bytes 2048
  425.6 3.4 pad_maximum_fusion.10
  430.7 14.2 %all_gather.138 = f32[8,1,32,192]{3,2,1,0:T(8,128)S(1)} all-gather(f32[1,1,32,192]{3,2,1,0:T(8,128)S(1)} %reshape.2807), channel_id=1, replica_groups=mesh['dom'=8,'four'=4] {'dom'}, dimensions={0}, use_global_device_ids=true | all-gather | bytes 221184 | tf_op jit(solution)/shard_map/all_gather | solution.py:189
  450.6 3.6 scatter-add.234
  458.1 5.8 scatter-add.236
  467.1 3.5 pad_maximum_fusion.5
  472.2 14.2 %all_gather.120 = f32[8,1,32,192]{3,2,1,0:T(8,128)S(1)} all-gather(f32[1,1,32,192]{3,2,1,0:T(8,128)S(1)} %reshape.2771), channel_id=1, replica_groups=mesh['dom'=8,'four'=4] {'dom'}, dimensions={0}, use_global_device_ids=true | all-gather | bytes 221184 | tf_op jit(solution)/shard_map/all_gather | solution.py:189
  496.8 5.3 scatter-add.196
  505.9 13.9 %all-reduce.68 = (f32[256]{0:T(256)S(1)}, f32[32]{0:T(128)S(1)}, f32[32]{0:T(128)S(1)}) all-reduce(f32[256]{0:T(256)S(1)} %dynamic-update-slice.164, f32[32]{0:T(128)S(1)} %get-tuple-element.630, f32[32]{0:T(128)S(1)} %get-tuple-element.635), channel_id=10, replica_groups=mesh['dom'=8,'four'=4] {'dom'}, use_global_device_ids=true, to_apply=%add.60 | all-reduce | flops 320 | bytes 2560
  520.0 3.4 fusion.20
  524.0 13.8 %all-reduce.67 = (f32[256]{0:T(256)S(1)}, f32[256]{0:T(256)S(1)}, f32[256]{0:T(256)S(1)}, f32[32]{0:T(128)S(1)}) all-reduce(f32[256]{0:T(256)S(1)} %dynamic-update-slice.165, f32[256]{0:T(256)S(1)} %dynamic-update-slice.159, f32[256]{0:T(256)S(1)} %dynamic-update-slice.160, ...), channel_id=11, replica_groups=mesh['dom'=8,'four'=4] {'dom'}, use_global_device_ids=true, to_apply=%add.61 | all-reduce | flops 800 | bytes 6400
  557.2 3.4 pad_maximum_fusion.11
  562.3 14.4 %all_gather.141 = f32[8,1,32,192]{3,2,1,0:T(8,128)S(1)} all-gather(f32[1,1,32,192]{3,2,1,0:T(8,128)S(1)} %reshape.2813), channel_id=1, replica_groups=mesh['dom'=8,'four'=4] {'dom'}, dimensions={0}, use_global_device_ids=true | all-gather | bytes 221184 | tf_op jit(solution)/shard_map/all_gather | solution.py:189
  589.6 5.8 scatter-add.244
  598.6 3.5 pad_maximum_fusion.6
  603.8 14.2 %all_gather.123 = f32[8,1,32,192]{3,2,1,0:T(8,128)S(1)} all-gather(f32[1,1,32,192]{3,2,1,0:T(8,128)S(1)} %reshape.2777), channel_id=1, replica_groups=mesh['dom'=8,'four'=4] {'dom'}, dimensions={0}, use_global_device_ids=true | all-gather | bytes 221184 | tf_op jit(solution)/shard_map/all_gather | solution.py:189
  628.4 5.3 scatter-add.204
  637.9 14.3 %all-reduce.57 = f32[256]{0:T(256)S(1)} all-reduce(f32[256]{0:T(256)S(1)} %dynamic-update-slice.161), channel_id=7, replica_groups=mesh['dom'=8,'four'=4] {'dom'}, use_global_device_ids=true, to_apply=%add.57 | all-reduce | flops 256 | bytes 2048
  661.8 3.4 pad_maximum_fusion.8
  666.9 14.2 %all_gather.129 = f32[8,1,32,192]{3,2,1,0:T(8,128)S(1)} all-gather(f32[1,1,32,192]{3,2,1,0:T(8,128)S(1)} %reshape.2789), channel_id=1, replica_groups=mesh['dom'=8,'four'=4] {'dom'}, dimensions={0}, use_global_device_ids=true | all-gather | bytes 221184 | tf_op jit(solution)/shard_map/all_gather | solution.py:189
  694.0 5.8 scatter-add.216
  702.9 13.9 %psum.89 = f32[32]{0:T(128)S(1)} all-reduce(f32[32]{0:T(128)S(1)} %multiply_reduce_fusion.5), channel_id=1, replica_groups=mesh['dom'=8,'four'=4] {'dom'}, use_global_device_ids=true, to_apply=%region_25.26 | all-reduce | flops 32 | bytes 256 | tf_op jit(solution)/shard_map/psum | solution.py:222
  719.7 13.7 %all-reduce.58 = f32[256]{0:T(256)S(1)} all-reduce(f32[256]{0:T(256)S(1)} %dynamic-update-slice.162), channel_id=8, replica_groups=mesh['dom'=8,'four'=4] {'dom'}, use_global_device_ids=true, to_apply=%add.58 | all-reduce | flops 256 | bytes 2048
  751.3 14.2 %all_gather.132 = f32[8,1,32,192]{3,2,1,0:T(8,128)S(1)} all-gather(f32[1,1,32,192]{3,2,1,0:T(8,128)S(1)} %reshape.2795), channel_id=1, replica_groups=mesh['dom'=8,'four'=4] {'dom'}, dimensions={0}, use_global_device_ids=true | all-gather | bytes 221184 | tf_op jit(solution)/shard_map/all_gather | solution.py:189
  777.6 5.8 scatter-add.224
  786.5 13.9 %all-reduce.66 = (f32[32]{0:T(128)S(1)}, f32[32]{0:T(128)S(1)}) all-reduce(f32[32]{0:T(128)S(1)} %get-tuple-element.634, f32[32]{0:T(128)S(1)} %multiply_reduce_fusion.4), channel_id=1, replica_groups=mesh['dom'=8,'four'=4] {'dom'}, use_global_device_ids=true, to_apply=%region_41.42 | all-reduce | flops 64 | bytes 512 | tf_op jit(solution)/shard_map/psum | solution.py:222
  800.5 3.4 fusion.23
  804.3 13.8 %all-reduce.65 = (f32[256]{0:T(256)S(1)}, f32[256]{0:T(256)S(1)}) all-reduce(f32[256]{0:T(256)S(1)} %dynamic-update-slice.166, f32[256]{0:T(256)S(1)} %dynamic-update-slice.163), channel_id=12, replica_groups=mesh['dom'=8,'four'=4] {'dom'}, use_global_device_ids=true, to_apply=%add.62 | all-reduce | flops 512 | bytes 4096
  840.6 3.8 pad_maximum_fusion.12
  846.1 14.2 %all_gather.144 = f32[8,1,32,192]{3,2,1,0:T(8,128)S(1)} all-gather(f32[1,1,32,192]{3,2,1,0:T(8,128)S(1)} %reshape.2819), channel_id=1, replica_groups=mesh['dom'=8,'four'=4] {'dom'}, dimensions={0}, use_global_device_ids=true | all-gather | bytes 221184 | tf_op jit(solution)/shard_map/all_gather | solution.py:189
  873.3 5.9 scatter-add.250
  888.9 14.2 %all_gather.135 = f32[8,1,32,192]{3,2,1,0:T(8,128)S(1)} all-gather(f32[1,1,32,192]{3,2,1,0:T(8,128)S(1)} %reshape.2801), channel_id=1, replica_groups=mesh['dom'=8,'four'=4] {'dom'}, dimensions={0}, use_global_device_ids=true | all-gather | bytes 221184 | tf_op jit(solution)/shard_map/all_gather | solution.py:189
  915.5 4.8 scatter-add.230
  926.6 13.9 %psum.94 = f32[32]{0:T(128)S(1)} all-reduce(f32[32]{0:T(128)S(1)} %get-tuple-element.638), channel_id=1, replica_groups=mesh['dom'=8,'four'=4] {'dom'}, use_global_device_ids=true, to_apply=%region_45.46 | all-reduce | flops 32 | bytes 256 | tf_op jit(solution)/shard_map/psum | solution.py:222
  943.6 13.8 %all-reduce.63 = f32[256]{0:T(256)S(1)} all-reduce(f32[256]{0:T(256)S(1)} %dynamic-update-slice.167), channel_id=13, replica_groups=mesh['dom'=8,'four'=4] {'dom'}, use_global_device_ids=true, to_apply=%add.63 | all-reduce | flops 256 | bytes 2048
  973.1 14.2 %all_gather.147 = f32[8,1,32,192]{3,2,1,0:T(8,128)S(1)} all-gather(f32[1,1,32,192]{3,2,1,0:T(8,128)S(1)} %reshape.2825), channel_id=1, replica_groups=mesh['dom'=8,'four'=4] {'dom'}, dimensions={0}, use_global_device_ids=true | all-gather | bytes 221184 | tf_op jit(solution)/shard_map/all_gather | solution.py:189
  995.6 5.3 scatter-add.256
  1002.8 14.1 %all-reduce.64 = (f32[32]{0:T(128)S(1)}, f32[32]{0:T(128)S(1)}, f32[32]{0:T(128)S(1)}) all-reduce(f32[32]{0:T(128)S(1)} %multiply_reduce_fusion, f32[32]{0:T(128)S(1)} %get-tuple-element.637, f32[32]{0:T(128)S(1)} %get-tuple-element.632), channel_id=1, replica_groups=mesh['dom'=8,'four'=4] {'dom'}, use_global_device_ids=true, to_apply=%region_49.50 | all-reduce | flops 96 | bytes 768 | tf_op jit(solution)/shard_map/psum | solution.py:222
  1017.0 3.3 multiply_subtract_fusion.2
  1020.9 3.4 multiply_subtract_fusion.1
  (634 shorter events, 418.4 us)
Async XLA Ops:
  5.3 11.0 %copy-start.35 = (f32[3,32,2304]{2,1,0:T(8,128)S(1)}, f32[3,32,2304]{2,1,0:T(8,128)}, u32[]{:S(2)}) copy-start(f32[3,32,2304]{2,1,0:T(8,128)} %param.111) | copy-start | bytes 2654212
  10.9 6.3 copy-start.48
  10.9 9.6 copy-start.50
  11.0 25.7 %all-to-all-start = ((f32[4,1,55296]{2,1,0:T(1,128)}), f32[4,1,55296]{2,1,0:T(1,128)}, u32[]{:S(2)}, u32[]{:S(2)}) async-start(f32[4,1,55296]{2,1,0:T(1,128)} %reshape.2967), calls=%async_computation | async-start | bytes 1769472 | tf_op jit(solution)/shard_map/all_to_all | solution.py:170
  31.4 2.0 copy-start.49
  56.4 5.3 copy-start.51
  56.4 6.6 copy-start.46
  56.4 35.8 %all-to-all-start.1 = ((f32[6,128,576]{2,0,1:T(8,128)}), f32[6,128,576]{2,0,1:T(8,128)}, u32[]{:S(2)}, u32[]{:S(2)}) async-start(f32[6,128,576]{2,0,1:T(8,128)} %copy.6841), calls=%async_computation.1 | async-start | bytes 5242880 | tf_op jit(solution)/shard_map/all_to_all | solution.py:173
  110.4 4.3 copy-start.45
  113.5 4.8 copy-start.34
  118.3 4.7 copy-start.47
  123.0 8.1 copy-start.29
  123.0 8.1 copy-start.30
  209.1 1.7 copy-start.26
  209.1 1.7 copy-start.37
  209.1 2.5 copy-start.36
  283.8 2.2 copy-start.27
  284.1 5.8 copy-start.6
  286.8 2.4 copy-start.19
  297.1 1.5 copy-start
  413.8 2.6 copy-start.8
  417.4 1.1 copy-start.28
  419.5 2.9 copy-start.1
  539.5 3.7 copy-start.24
  543.2 3.6 copy-start.40
  545.1 2.4 copy-start.9
  545.1 2.4 copy-start.25
  545.2 2.4 copy-start.42
  551.1 2.9 copy-start.2
  652.6 2.6 copy-start.5
  657.1 1.5 copy-start.4
  735.1 2.6 copy-start.18
  774.9 25.5 %copy-start.3 = (f32[1,32,48,48]{2,1,3,0:T(8,128)S(1)}, f32[1,32,48,48]{2,1,3,0:T(8,128)}, u32[]{:S(2)}) copy-start(f32[1,32,48,48]{2,1,3,0:T(8,128)} %constant_dynamic-update-slice_fusion.6) | copy-start | bytes 884740
  818.1 2.7 copy-start.32
  820.9 4.3 copy-start.10
  821.7 3.5 copy-start.21
  825.2 3.4 copy-start.43
  825.2 3.4 copy-start.44
  827.0 130.5 %copy-start.11 = (f32[1,32,48,48]{2,3,1,0:T(8,128)}, f32[1,32,48,48]{2,3,1,0:T(8,128)S(1)}, u32[]{:S(2)}) copy-start(f32[1,32,48,48]{2,3,1,0:T(8,128)S(1)} %multiply_add_fusion.2) | copy-start | bytes 884740
  828.6 1.6 copy-start.22
  835.9 1.5 copy-start.15
  884.3 1.5 copy-start.13
  958.8 2.7 copy-start.16
  962.6 1.5 copy-start.12
  962.6 1.8 copy-start.20
  993.2 23.8 %copy-start.7 = (f32[1,32,48,48]{2,1,3,0:T(8,128)S(1)}, f32[1,32,48,48]{2,1,3,0:T(8,128)}, u32[]{:S(2)}) copy-start(f32[1,32,48,48]{2,1,3,0:T(8,128)} %copy-done.6) | copy-start | bytes 884740
  1017.0 3.9 copy-start.14
  1017.0 3.9 copy-start.17
  1017.0 3.9 copy-start.23
  1017.0 3.9 copy-start.31
  1017.0 3.9 copy-start.33
  1017.0 3.9 copy-start.38
  1017.0 3.9 copy-start.39
  1026.5 3.2 copy-start.41
